TPU v7x, 32 devices: a whole 2x2x4 slice. The times are simulated.
32 devices in a mesh: runs: 2 (over x), modes: 16 (over z, y, core).
Axes of the slice: x: 2, y: 2, z: 4, core: 2. Of those that a mesh axis runs over, the one named last changes fastest.
Arguments:
- amplitudes: float32 [8192, 2, 5, 512], P(('runs', 'modes')), parts along dimension 0, may hold values from -6 to 6
- mode_table: int32 [4096, 2], replicated, may hold values from 0 to 127, as said below
- slab_map: int32 [8], replicated, may hold values from 0 to 7, each once
- base_flow: float32 [1024], P('runs'), parts along dimension 0, may hold values from 0 to 1.5
- base_coupling: float32 [50, 512], P('runs'), parts along dimension 0, may hold values from -0.36 to 0.36
- slab_inverse: float32 [8, 64, 64], replicated
- wall_operator: float32 [64, 64], replicated, may hold values from -0.75 to 0.75
Outputs:
- marched: float32 [8192, 2, 5, 512], P(('runs', 'modes')), parts along dimension 0
There are 2 independent parts, one for each index of `runs`. A program takes and returns all parts, laid end to end along the dimension named above; an argument that names none is the same for every part. Nothing has to cross between parts.
Inputs may be any that keep to these rules, and one draw needn't show every extreme that they name: `mode_table`: every cell of the 32 x 128 grid is named by exactly one mode; column 0 lies in 0 to 31. `slab_map`: each subdomain has its own slot.
All inputs are finite; a program needn't handle non-finite values.
Results may differ from a plain program's by a relative error of at most 0.0003.
Values sent between devices are 32-bit elements; how exact they have to be, the bound alone decides.
No kernel may reach another device: no remote copies, remote signals or barrier semaphores. Data moves between devices by JAX's collectives and lax.ppermute only.
A program may use at most 192 MiB of HBM per device.

v0:
```python
import math
import jax
import jax.numpy as jnp
from jax import lax
from jax.sharding import PartitionSpec as P

M = 4096
NB = 128
SWEEPS = 3
NW = 32
precise = lax.Precision.HIGHEST
omega_step = 0.01
phase_gain = 0.2
march_step = 0.2
coupling = 0.3


def twiddle(length):
    counter = jnp.arange(length, dtype=jnp.int32)
    product = counter[:, None] * counter[None, :] % length
    angles = product.astype(jnp.float32) * (2.0 * math.pi / length)
    return (jnp.cos(angles), jnp.sin(angles))


def mode_tables(mode_table):
    omega_index = mode_table[:, 0]
    beta_index = mode_table[:, 1]
    signed = jnp.where(beta_index >= NB // 2, beta_index - NB, beta_index)
    wavenum = 2.0 * signed.astype(jnp.float32) / NB
    frequency = omega_step * omega_index.astype(jnp.float32)
    grid_pos = omega_index * NB + beta_index
    mode_at = jnp.zeros((M,), jnp.int32).at[grid_pos].set(jnp.arange(M, dtype=jnp.int32))
    return (wavenum, frequency, grid_pos, mode_at)


def synthesize(real_part, imag_part, tables, factor):
    cos_omega, sin_omega, cos_beta, sin_beta = tables
    mixed_re = jnp.einsum("...wb,bz->...wz", real_part, cos_beta, precision=precise) - jnp.einsum(
        "...wb,bz->...wz", imag_part, sin_beta, precision=precise
    )
    mixed_im = jnp.einsum("...wb,bz->...wz", real_part, sin_beta, precision=precise) + jnp.einsum(
        "...wb,bz->...wz", imag_part, cos_beta, precision=precise
    )
    physical = jnp.einsum("...wz,wt->...tz", mixed_re, cos_omega, precision=precise) - jnp.einsum(
        "...wz,wt->...tz", mixed_im, sin_omega, precision=precise
    )
    return physical * factor


def analyze(physical, tables, factor):
    cos_omega, sin_omega, cos_beta, sin_beta = tables
    half_re = jnp.einsum("...tz,zb->...tb", physical, cos_beta, precision=precise)
    half_im = -jnp.einsum("...tz,zb->...tb", physical, sin_beta, precision=precise)
    coef_re = jnp.einsum("...tb,tw->...wb", half_re, cos_omega, precision=precise) + jnp.einsum(
        "...tb,tw->...wb", half_im, sin_omega, precision=precise
    )
    coef_im = jnp.einsum("...tb,tw->...wb", half_im, cos_omega, precision=precise) - jnp.einsum(
        "...tb,tw->...wb", half_re, sin_omega, precision=precise
    )
    return (coef_re * factor, coef_im * factor)


def forcing(normal_vel, spanwise_vel, wall_grad, span_grad, tables, factor):
    vel_v = synthesize(normal_vel[0], normal_vel[1], tables, factor)
    vel_w = synthesize(spanwise_vel[0], spanwise_vel[1], tables, factor)
    grad_y = synthesize(wall_grad[0], wall_grad[1], tables, factor)
    grad_z = synthesize(span_grad[0], span_grad[1], tables, factor)
    product = -(vel_v[None] * grad_y + vel_w[None] * grad_z)
    return analyze(product, tables, factor)


def wall_derivative(values, wall_operator):
    slab_width = wall_operator.shape[0]
    slab_count = values.shape[3] // slab_width
    blocks = values.reshape(values.shape[:3] + (slab_count, slab_width))
    return jnp.einsum("ij,abcsj->abcsi", wall_operator, blocks, precision=precise).reshape(
        values.shape
    )


def interface_table(slab_map, slab_count, slab_width):
    inverse = (
        jnp.zeros((slab_count,), jnp.int32)
        .at[slab_map]
        .set(jnp.arange(slab_count, dtype=jnp.int32))
    )
    position = jnp.arange(slab_count * slab_width, dtype=jnp.int32)
    slot_of = position // slab_width
    within = position % slab_width
    domain = inverse[slot_of]
    below = slab_map[jnp.maximum(domain - 1, 0)] * slab_width + (slab_width - 1)
    above = slab_map[jnp.minimum(domain + 1, slab_count - 1)] * slab_width
    lower_ok = (within == 0) & (domain > 0)
    upper_ok = (within == slab_width - 1) & (domain < slab_count - 1)
    source = jnp.where(lower_ok, below, jnp.where(upper_ok, above, 0))
    weight = (lower_ok | upper_ok).astype(jnp.float32)
    return (source, weight)


def relaxation(iterate, right_side, rotation, matrix, slab_inverse, source, weight):
    slab_count = slab_inverse.shape[0]
    slab_width = slab_inverse.shape[1]
    coupled = jnp.einsum("kjy,acjy->acky", matrix, iterate, precision=precise)
    applied = jnp.stack(
        [
            coupled[:, 0] - rotation[:, None, :] * iterate[:, 1],
            coupled[:, 1] + rotation[:, None, :] * iterate[:, 0],
        ],
        1,
    )
    rims = jnp.take(iterate, source, axis=3) * weight
    residual_in = right_side - applied + coupling * rims
    blocks = residual_in.reshape(iterate.shape[:3] + (slab_count, slab_width))
    return jnp.einsum("sij,acvsj->acvsi", slab_inverse, blocks, precision=precise).reshape(
        iterate.shape
    )


def local(amplitudes, mode_table, slab_map, base_flow, base_coupling, slab_inverse, wall_operator):
    local_modes = amplitudes.shape[0]
    wall_points = amplitudes.shape[3]
    groups = lax.axis_size("modes")
    point_share = wall_points // groups
    wavenum, frequency, grid_pos, mode_at = mode_tables(mode_table)
    first_mode = lax.axis_index("modes") * local_modes
    wave_local = lax.dynamic_slice_in_dim(wavenum, first_mode, local_modes)
    freq_local = lax.dynamic_slice_in_dim(frequency, first_mode, local_modes)
    tables = twiddle(NW) + twiddle(NB)
    factor = 1.0 / math.sqrt(M)
    source, weight = interface_table(slab_map, slab_inverse.shape[0], slab_inverse.shape[1])
    matrix = base_coupling.reshape(5, 5, wall_points)
    gradient = wall_derivative(amplitudes, wall_operator)
    span = jnp.stack(
        [
            -wave_local[:, None, None] * amplitudes[:, 1],
            wave_local[:, None, None] * amplitudes[:, 0],
        ],
        1,
    )
    fields = jnp.concatenate([amplitudes[:, :, 2:4], gradient, span], 2)
    field_count = fields.shape[2]
    channels = 2 * field_count
    outgoing = jnp.transpose(
        fields.reshape(local_modes, channels, groups, point_share), (1, 2, 3, 0)
    ).reshape(channels, groups, point_share * local_modes)
    incoming = lax.all_to_all(outgoing, "modes", split_axis=1, concat_axis=1, tiled=True)
    by_mode = jnp.transpose(
        incoming.reshape(channels, groups, point_share, local_modes), (0, 2, 1, 3)
    ).reshape(channels, point_share, M)
    gridded = by_mode[..., mode_at].reshape(2, field_count, point_share, NW, NB)
    normal_vel = gridded[:, 0]
    spanwise_vel = gridded[:, 1]
    wall_grad = gridded[:, 2:7]
    span_grad = gridded[:, 7:12]
    mean_crossflow = lax.all_gather(spanwise_vel[0, :, 0, 0], "modes", axis=0, tiled=True)
    coef_re, coef_im = forcing(normal_vel, spanwise_vel, wall_grad, span_grad, tables, factor)
    packed = jnp.stack([coef_re, coef_im], 0).reshape(10, point_share, M)[..., grid_pos]
    sendback = jnp.transpose(
        packed.reshape(10, point_share, groups, local_modes), (0, 2, 1, 3)
    ).reshape(10, groups, point_share * local_modes)
    returned = lax.all_to_all(sendback, "modes", split_axis=1, concat_axis=1, tiled=True)
    nonlinear = jnp.transpose(
        returned.reshape(10, groups, point_share, local_modes), (3, 0, 1, 2)
    ).reshape(local_modes, 2, 5, wall_points)
    crossflow = base_flow + mean_crossflow
    rotation = phase_gain * wave_local[:, None] * crossflow[None, :] - freq_local[:, None]
    right_side = amplitudes + march_step * nonlinear
    iterate = amplitudes
    for sweep_index in range(SWEEPS):
        iterate = relaxation(iterate, right_side, rotation, matrix, slab_inverse, source, weight)
    return iterate


def solution(mesh):
    return jax.shard_map(
        local,
        mesh=mesh,
        in_specs=(
            P(("runs", "modes"), None, None, None),
            P(),
            P(),
            P("runs"),
            P("runs", None),
            P(),
            P(),
        ),
        out_specs=P(("runs", "modes"), None, None, None),
        check_vma=False,
    )
```

profile of v0, /device:TPU:16, one launch (start us, length us, event | category | flops | bytes accessed | tf_op | source)
XLA Modules:
  0.0 1126.5 jit_solution(16035738039939335785)
XLA Ops:
  0.0 9.0 copy.115
  9.0 8.7 copy.102
  19.0 4.6 slice.154
  23.6 4.1 slice_multiply_fusion.5
  27.8 5.3 fusion.90
  36.3 7.8 maximum_maximum_fusion
  44.1 17.6 %copy.106 = f32[256,2,12,512]{0,3,2,1:T(8,128)} copy(f32[256,2,12,512]{0,2,1,3:T(8,128)} %maximum_maximum_fusion) | data formatting | bytes 25165824 | tf_op jit(solution)/shard_map/concatenate | solution.py:140
  61.7 14.2 %reshape.217 = f32[24,16,8192]{2,1,0:T(8,128)} reshape(f32[24,16,32,256]{3,2,1,0:T(8,128)} %bitcast.293) | data formatting | bytes 25165824 | tf_op jit(solution)/shard_map/reshape | solution.py:145
  75.9 16.4 %copy.107 = f32[24,16,8192]{2,0,1:T(8,128)} copy(f32[24,16,8192]{2,1,0:T(8,128)} %reshape.217) | data formatting | bytes 25165824 | tf_op jit(solution)/shard_map/reshape | solution.py:145
  92.3 6.2 all-to-all-start
  98.4 15.7 %scatter_custom_fusion = s32[4096]{0:T(1024)S(1)} fusion(s32[4096]{0:T(1024)S(1)} %bitcast.308, s32[4096]{0:T(1024)S(1)} %iota.30, s32[]{:T(128)} %constant.98.clone.1), kind=kCustom, calls=%fused_computation.165 | custom fusion | bytes 16388 | tf_op jit(solution)/shard_map/scatter | solution.py:32
  114.2 256.7 %all-to-all-done = f32[24,16,8192]{2,0,1:T(8,128)} async-done(((f32[24,16,8192]{2,0,1:T(8,128)}), f32[24,16,8192]{2,0,1:T(8,128)}, u32[]{:S(2)}, u32[]{:S(2)}) %all-to-all-start) | async-done | bytes 12582944 | tf_op jit(solution)/shard_map/all_to_all | solution.py:146
  370.9 14.6 %copy.146 = f32[48,8,32,256]{3,2,1,0:T(8,128)} copy(f32[48,8,32,256]{3,1,2,0:T(8,128)} %bitcast.101) | data formatting | bytes 25165824
  385.5 29.6 %copy.138 = f32[24,32,16,256]{1,0,3,2:T(8,128)} copy(f32[24,32,16,256]{3,1,0,2:T(8,128)} %bitcast.294) | data formatting | bytes 25165824 | tf_op jit(solution)/shard_map/reshape | solution.py:149
  415.1 86.4 %gather_fusion = f32[4096,24,32]{2,1,0:T(8,128)} fusion(f32[24,32,4096]{1,0,2:T(8,128)} %bitcast.291, s32[4096]{0:T(1024)S(1)} %fusion.115), kind=kCustom, calls=%fused_computation.3 | custom fusion | bytes 25182208 | tf_op jit(solution)/shard_map/gather | solution.py:150
  501.5 32.3 %copy.110 = f32[24,32,4096]{2,1,0:T(8,128)} copy(f32[24,32,4096]{1,0,2:T(8,128)} %bitcast.292) | data formatting | bytes 25165824 | tf_op jit(solution)/shard_map/gather | solution.py:150
  533.8 12.0 %copy.147 = f32[96,8,32,128]{3,2,1,0:T(8,128)} copy(f32[96,8,32,128]{3,1,2,0:T(8,128)} %bitcast.295) | data formatting | bytes 25165824
  554.0 4.3 fusion.26
  558.2 4.3 fusion.28
  592.3 3.5 fusion.17
  614.5 6.8 reshape.221
  621.3 22.0 %copy.111 = f32[10,32,4096]{1,0,2:T(8,128)} copy(f32[10,32,4096]{2,1,0:T(8,128)} %reshape.221) | data formatting | bytes 10485760 | tf_op jit(solution)/shard_map/reshape | solution.py:157
  643.3 78.3 %gather_fusion.1 = f32[4096,10,32]{2,1,0:T(8,128)} fusion(f32[10,32,4096]{1,0,2:T(8,128)} %copy.111, s32[4096]{0:T(1024)S(1)} %broadcast_clamp_fusion), kind=kCustom, calls=%fused_computation.4 | custom fusion | bytes 10502144 | tf_op jit(solution)/shard_map/gather | solution.py:157
  721.6 21.3 %copy.112 = f32[10,32,16,256]{3,1,2,0:T(8,128)} copy(f32[10,32,16,256]{1,0,3,2:T(8,128)} %bitcast.296) | data formatting | bytes 10485760 | tf_op jit(solution)/shard_map/reshape | solution.py:159
  743.0 6.9 reshape.223
  749.9 9.0 copy.113
  758.9 4.8 all-to-all-start.1
  765.0 4.4 compare_select_fusion.10
  770.8 4.4 compare_select_fusion.4
  775.2 5.8 compare_and_fusion
  781.0 7.8 gather_fusion.2
  791.6 11.8 %convolution_bitcast_fusion.2 = f32[256,2,5,512]{0,2,1,3:T(8,128)} fusion(f32[256,2,5,512]{0,2,1,3:T(8,128)} %copy.115, f32[5,5,512,1]{1,0,3,2:T(8,128)S(1)} %copy.134), kind=kOutput, calls=%fused_computation.43 | convolution fusion | flops 78643200 | bytes 10536960 | tf_op jit(solution)/shard_map/kjy,acjy->acky/dot_general | solution.py:103
  805.3 159.1 %all-reduce = f32[512]{0:T(512)S(1)} all-reduce(f32[512]{0:T(512)S(1)} %dynamic-update-slice), channel_id=2, replica_groups=mesh['runs'=2,'modes'=16] {'modes'}, use_global_device_ids=true, to_apply=%add | all-reduce | flops 512 | bytes 4096 | tf_op jit(solution)/shard_map/all_gather | solution.py:155
  965.3 10.0 slice_subtract_fusion
  975.3 6.8 copy_multiply_fusion
  986.9 11.0 fusion
  997.9 8.4 fusion.38
  1012.8 9.8 convolution_bitcast_fusion.1
  1022.6 7.8 gather_fusion.3
  1030.4 8.8 fusion.15
  1041.6 10.4 fusion.1
  1052.0 8.4 fusion.41
  1066.9 9.9 convolution_bitcast_fusion
  1076.8 7.9 gather_fusion.4
  1084.6 8.7 fusion.13
  1095.7 10.5 fusion.2
  1106.1 8.4 fusion.44
  1117.2 8.8 copy.128
  (110 shorter events, 93.7 us)
Async XLA Ops:
  0.0 997.9 %copy-start = (f32[8,64,64]{2,1,0:T(8,128)S(1)}, f32[8,64,64]{2,1,0:T(8,128)}, u32[]{:S(2)}) copy-start(f32[8,64,64]{2,1,0:T(8,128)} %param.14) | copy-start | bytes 393220
  9.0 8.7 copy-start.13
  19.0 8.8 slice-start.4
  23.6 4.1 slice-start.5
  23.6 4.1 copy-start.12
  92.3 278.6 %all-to-all-start = ((f32[24,16,8192]{2,0,1:T(8,128)}), f32[24,16,8192]{2,0,1:T(8,128)}, u32[]{:S(2)}, u32[]{:S(2)}) async-start(f32[24,16,8192]{2,0,1:T(8,128)} %copy.107), calls=%async_computation | async-start | bytes 25165824 | tf_op jit(solution)/shard_map/all_to_all | solution.py:146
  547.7 14.8 %copy-start.3 = (f32[96,8,32,128]{3,2,1,0:T(8,128)S(1)}, f32[96,8,32,128]{3,2,1,0:T(8,128)}, u32[]{:S(2)}) copy-start(f32[96,8,32,128]{3,2,1,0:T(8,128)} %copy.147) | copy-start | bytes 37748740
  758.8 4.8 copy-start.14
  758.9 216.5 %all-to-all-start.1 = ((f32[10,16,8192]{2,0,1:T(8,128)}), f32[10,16,8192]{2,0,1:T(8,128)}, u32[]{:S(2)}, u32[]{:S(2)}) async-start(f32[10,16,8192]{2,0,1:T(8,128)} %copy.113), calls=%async_computation.1 | async-start | bytes 16777216 | tf_op jit(solution)/shard_map/all_to_all | solution.py:161
  781.0 7.8 copy-start.11
  781.0 8.6 copy-start.17
  791.6 172.8 %copy-start.16 = (f32[512]{0:T(512)S(1)}, f32[512]{0:T(512)}, u32[]{:S(2)}) copy-start(f32[512]{0:T(512)} %param.12) | copy-start | bytes 6148
  791.6 172.8 %copy-start.15 = (f32[256]{0:T(256)S(1)}, f32[256]{0:T(256)}, u32[]{:S(2)}) copy-start(f32[256]{0:T(256)} %get-tuple-element.8) | copy-start | bytes 3076
  964.5 0.9 copy-start.9
  982.1 2.2 copy-start.7
  982.1 4.8 copy-start.8
  984.0 14.0 %copy-start.4 = (f32[20,8,32,256]{3,2,1,0:T(8,128)}, f32[20,8,32,256]{3,2,1,0:T(8,128)S(1)}, u32[]{:S(2)}) copy-start(f32[20,8,32,256]{3,2,1,0:T(8,128)S(1)} %copy.148) | copy-start | bytes 15728644
  1009.5 3.3 copy-start.2
  1022.6 16.6 %slice-start = ((s8[5242880]{0:T(1024)(128)(4,1)}), s8[1048576]{0:T(1024)(128)(4,1)S(1)}, s32[]{:S(2)}) async-start(s8[5242880]{0:T(1024)(128)(4,1)} %bitcast.285), calls=%async_computation.2 | async-start | bytes 2097152
  1030.4 8.8 slice-start.1
  1030.4 11.2 copy-start.6
  1063.6 3.3 copy-start.1
  1076.7 7.9 copy-start.10
  1076.7 16.6 %slice-start.2 = ((s8[5242880]{0:T(1024)(128)(4,1)}), s8[1048576]{0:T(1024)(128)(4,1)S(1)}, s32[]{:S(2)}) async-start(s8[5242880]{0:T(1024)(128)(4,1)} %bitcast.288), calls=%async_computation.4 | async-start | bytes 2097152
  1084.6 8.7 slice-start.3
  1084.6 11.0 copy-start.5
where the time goes:
time: 1140 us; the launch traced here: 1130 us
  local copies, waits for them, and re-layouts  472 us (41%)
  waiting for transfers between devices  257 us (23%)
  blocking collectives  159 us (14%)
  matrix products  127 us (11%)
  other arithmetic  98.3 us (9%)
    all_to_all x1, waiting for transfers between devices, local(): lax.all_to_all(outgoing, 'modes', split_axis=1, concat_axis=1, tiled=True)  257 us
    all_gather x1, blocking collectives, local(): lax.all_gather(spanwise_vel[0, :, 0, 0], 'modes', axis=0, tiled=True)  159 us
    gather x2, local copies, waits for them, and re-layouts, local(): gridded = by_mode[..., mode_at].reshape(2, field_count, point_share, NW, NB)  119 us
    gather x1, local copies, waits for them, and re-layouts, local(): jnp.stack([coef_re, coef_im], 0).reshape(10, point_share, M)[..., grid_pos]  78.3 us
    unnamed x56, local copies, waits for them, and re-layouts  62 us
    add x3, other arithmetic, relaxation(): residual_in = right_side - applied + coupling * rims  31.9 us
    dot_general x3, matrix products, relaxation(): coupled = jnp.einsum('kjy,acjy->acky', matrix, iterate, precision=precise)  31.5 us
    reshape x2, local copies, waits for them, and re-layouts, local(): outgoing = jnp.transpose(fields.reshape(local_modes, channels, groups, po...  30.6 us
  transfers between devices with their start and end apart: 2, of which 1 were waited for; matrix products, arithmetic and copies ran while one was open for 6% of the time, Pallas kernels for 0%

commit v1 on v0

--- a/solution.py
+++ b/solution.py
@@ -13,6 +13,13 @@
 phase_gain = 0.2
 march_step = 0.2
 coupling = 0.3
+
+
+def exchange_blocks(shard, axis, split, join):
+    devices = lax.axis_size(axis)
+    parts = jnp.stack(jnp.split(shard, devices, axis=split), axis=0)
+    parts = lax.all_to_all(parts, axis, split_axis=0, concat_axis=0)
+    return jnp.concatenate(parts, axis=join)
 
 
 def twiddle(length):
@@ -143,7 +150,7 @@
     outgoing = jnp.transpose(
         fields.reshape(local_modes, channels, groups, point_share), (1, 2, 3, 0)
     ).reshape(channels, groups, point_share * local_modes)
-    incoming = lax.all_to_all(outgoing, "modes", split_axis=1, concat_axis=1, tiled=True)
+    incoming = exchange_blocks(outgoing, "modes", 1, 1)
     by_mode = jnp.transpose(
         incoming.reshape(channels, groups, point_share, local_modes), (0, 2, 1, 3)
     ).reshape(channels, point_share, M)

time: 1140 us -> 1240 us (1.088)
  local copies, waits for them, and re-layouts: 472 us -> 567 us
    unnamed x56 -> x71, local copies, waits for them, and re-layouts: 62 us -> 130 us
    reshape x0 -> x1, local copies, waits for them, and re-layouts: none -> 38.7 us  [exchange_blocks(): return jnp.concatenate(parts, axis=join)]
    reshape x2 -> x1, local copies, waits for them, and re-layouts: 30.6 us -> 14.2 us  [local(): outgoing = jnp.transpose(fields.reshape(local_modes, channels, groups, po...]
  transfers between devices with their start and end apart: 2 -> 2, of which waited for: 1 -> 1; matrix products, arithmetic and copies ran while one was open for 6% -> 5% of each run, Pallas kernels for 0% -> 0%
where the time goes in v1:
time: 1240 us; the launch traced here: 1220 us
  local copies, waits for them, and re-layouts  567 us (46%)
  waiting for transfers between devices  257 us (21%)
  blocking collectives  159 us (13%)
  matrix products  127 us (10%)
  other arithmetic  98.2 us (8%)
    all_to_all x1, waiting for transfers between devices, exchange_blocks(): parts = lax.all_to_all(parts, axis, split_axis=0, concat_axis=0)  257 us
    all_gather x1, blocking collectives, local(): lax.all_gather(spanwise_vel[0, :, 0, 0], 'modes', axis=0, tiled=True)  159 us
    unnamed x71, local copies, waits for them, and re-layouts  130 us
    gather x2, local copies, waits for them, and re-layouts, local(): gridded = by_mode[..., mode_at].reshape(2, field_count, point_share, NW, NB)  119 us
    gather x1, local copies, waits for them, and re-layouts, local(): jnp.stack([coef_re, coef_im], 0).reshape(10, point_share, M)[..., grid_pos]  78.3 us
    reshape x1, local copies, waits for them, and re-layouts, exchange_blocks(): return jnp.concatenate(parts, axis=join)  38.7 us
    add x3, other arithmetic, relaxation(): residual_in = right_side - applied + coupling * rims  31.9 us
    dot_general x3, matrix products, relaxation(): coupled = jnp.einsum('kjy,acjy->acky', matrix, iterate, precision=precise)  31.5 us
  transfers between devices with their start and end apart: 2, of which 1 were waited for; matrix products, arithmetic and copies ran while one was open for 5% of the time, Pallas kernels for 0%

profile of v1, /device:TPU:16, one launch (start us, length us, event | category | flops | bytes accessed | tf_op | source)
XLA Modules:
  0.0 1221.4 jit_solution(16425496656666335703)
XLA Ops:
  0.0 9.0 copy.113
  9.0 8.7 copy.101
  19.0 4.6 slice.154
  27.8 5.3 fusion.106
  36.4 7.7 maximum_maximum_fusion
  44.1 17.6 %copy.105 = f32[256,2,12,512]{0,3,2,1:T(8,128)} copy(f32[256,2,12,512]{0,2,1,3:T(8,128)} %maximum_maximum_fusion) | data formatting | bytes 25165824 | tf_op jit(solution)/shard_map/concatenate | solution.py:147
  61.7 14.2 %reshape.217 = f32[24,16,8192]{2,1,0:T(8,128)} reshape(f32[24,16,32,256]{3,2,1,0:T(8,128)} %bitcast.359) | data formatting | bytes 25165824 | tf_op jit(solution)/shard_map/reshape | solution.py:152
  84.6 4.6 fusion.70
  89.2 4.6 fusion.69
  103.0 4.6 fusion.66
  125.4 4.6 fusion.61
  134.6 4.6 fusion.59
  143.7 4.7 fusion.57
  148.4 6.5 all-to-all-start
  154.9 15.5 %scatter_custom_fusion = s32[4096]{0:T(1024)S(1)} fusion(s32[4096]{0:T(1024)S(1)} %bitcast.375, s32[4096]{0:T(1024)S(1)} %iota.30, s32[]{:T(128)} %constant.98.clone.1), kind=kCustom, calls=%fused_computation.198 | custom fusion | bytes 16388 | tf_op jit(solution)/shard_map/scatter | solution.py:39
  170.4 256.7 %all-to-all-done = f32[16,24,1,8192]{3,2,1,0:T(1,128)} async-done(((f32[16,24,1,8192]{3,2,1,0:T(1,128)}), f32[16,24,1,8192]{3,2,1,0:T(1,128)}, u32[]{:S(2)}, u32[]{:S(2)}) %all-to-all-start) | async-done | bytes 12582944 | tf_op jit(solution)/shard_map/all_to_all | solution.py:21
  427.2 38.7 %bitcast_reduce_fusion = f32[24,16,8192]{2,0,1:T(8,128)} fusion(f32[16,24,1,8192]{3,2,1,0:T(1,128)} %all-to-all-done), kind=kLoop, calls=%fused_computation.8 | loop fusion | bytes 25165824 | tf_op jit(solution)/shard_map/reshape | solution.py:22
  465.9 14.6 %copy.144 = f32[48,8,32,256]{3,2,1,0:T(8,128)} copy(f32[48,8,32,256]{3,1,2,0:T(8,128)} %bitcast.360) | data formatting | bytes 25165824
  480.5 29.6 %copy.136 = f32[24,32,16,256]{1,0,3,2:T(8,128)} copy(f32[24,32,16,256]{3,1,0,2:T(8,128)} %bitcast.361) | data formatting | bytes 25165824 | tf_op jit(solution)/shard_map/reshape | solution.py:156
  510.1 86.3 %gather_fusion = f32[4096,24,32]{2,1,0:T(8,128)} fusion(f32[24,32,4096]{1,0,2:T(8,128)} %bitcast.357, s32[4096]{0:T(1024)S(1)} %get-tuple-element.38), kind=kCustom, calls=%fused_computation.3 | custom fusion | bytes 25182208 | tf_op jit(solution)/shard_map/gather | solution.py:157
  596.4 32.3 %copy.108 = f32[24,32,4096]{2,1,0:T(8,128)} copy(f32[24,32,4096]{1,0,2:T(8,128)} %bitcast.358) | data formatting | bytes 25165824 | tf_op jit(solution)/shard_map/gather | solution.py:157
  628.7 12.0 copy.145
  709.4 6.8 reshape.221
  716.3 22.0 %copy.109 = f32[10,32,4096]{1,0,2:T(8,128)} copy(f32[10,32,4096]{2,1,0:T(8,128)} %reshape.221) | data formatting | bytes 10485760 | tf_op jit(solution)/shard_map/reshape | solution.py:164
  738.2 78.3 %gather_fusion.1 = f32[4096,10,32]{2,1,0:T(8,128)} fusion(f32[10,32,4096]{1,0,2:T(8,128)} %copy.109, s32[4096]{0:T(1024)S(1)} %get-tuple-element.39), kind=kCustom, calls=%fused_computation.4 | custom fusion | bytes 10502144 | tf_op jit(solution)/shard_map/gather | solution.py:164
  816.6 21.3 %copy.110 = f32[10,32,16,256]{3,1,2,0:T(8,128)} copy(f32[10,32,16,256]{1,0,3,2:T(8,128)} %bitcast.363) | data formatting | bytes 10485760 | tf_op jit(solution)/shard_map/reshape | solution.py:166
  837.9 6.9 reshape.223
  844.8 9.0 copy.111
  853.8 4.8 all-to-all-start.1
  870.9 5.7 compare_and_fusion
  876.7 7.8 gather_fusion.2
  886.3 11.8 convolution_bitcast_fusion.2
  900.0 159.2 %all-reduce = f32[512]{0:T(512)S(1)} all-reduce(f32[512]{0:T(512)S(1)} %dynamic-update-slice), channel_id=2, replica_groups=mesh['runs'=2,'modes'=16] {'modes'}, use_global_device_ids=true, to_apply=%add | all-reduce | flops 512 | bytes 4096 | tf_op jit(solution)/shard_map/all_gather | solution.py:162
  1060.3 10.0 slice_subtract_fusion
  1070.2 6.8 copy_multiply_fusion
  1081.8 11.0 fusion
  1092.9 8.4 fusion.38
  1107.7 9.8 convolution_bitcast_fusion.1
  1117.5 7.8 gather_fusion.3
  1125.4 8.8 fusion.15
  1136.5 10.4 fusion.1
  1146.9 8.4 fusion.41
  1161.8 9.9 convolution_bitcast_fusion
  1171.6 7.9 gather_fusion.4
  1179.5 8.7 fusion.13
  1190.5 10.5 fusion.2
  1201.0 8.4 fusion.44
  1212.1 8.8 copy.126
  (125 shorter events, 163.4 us)
Async XLA Ops:
  0.0 1092.9 %copy-start = (f32[8,64,64]{2,1,0:T(8,128)S(1)}, f32[8,64,64]{2,1,0:T(8,128)}, u32[]{:S(2)}) copy-start(f32[8,64,64]{2,1,0:T(8,128)} %param.14) | copy-start | bytes 393220
  9.0 8.7 copy-start.13
  19.0 8.8 slice-start.4
  23.6 4.1 slice-start.5
  23.6 4.1 copy-start.12
  148.4 278.8 %all-to-all-start = ((f32[16,24,1,8192]{3,2,1,0:T(1,128)}), f32[16,24,1,8192]{3,2,1,0:T(1,128)}, u32[]{:S(2)}, u32[]{:S(2)}) async-start(f32[16,24,1,8192]{3,2,1,0:T(1,128)} %fusion.57), calls=%async_computation | async-start | bytes 25165824 | tf_op jit(solution)/shard_map/all_to_all | solution.py:21
  640.7 16.7 %copy-start.3 = (f32[96,8,32,128]{3,2,1,0:T(8,128)S(1)}, f32[96,8,32,128]{3,2,1,0:T(8,128)}, u32[]{:S(2)}) copy-start(f32[96,8,32,128]{3,2,1,0:T(8,128)} %copy.145) | copy-start | bytes 37748740
  853.8 4.9 copy-start.11
  853.8 5.7 copy-start.14
  853.8 216.4 %all-to-all-start.1 = ((f32[10,16,8192]{2,0,1:T(8,128)}), f32[10,16,8192]{2,0,1:T(8,128)}, u32[]{:S(2)}, u32[]{:S(2)}) async-start(f32[10,16,8192]{2,0,1:T(8,128)} %copy.111), calls=%async_computation.1 | async-start | bytes 16777216 | tf_op jit(solution)/shard_map/all_to_all | solution.py:168
  876.6 7.8 copy-start.17
  886.3 172.9 %copy-start.16 = (f32[512]{0:T(512)S(1)}, f32[512]{0:T(512)}, u32[]{:S(2)}) copy-start(f32[512]{0:T(512)} %param.12) | copy-start | bytes 6148
  886.3 172.9 %copy-start.15 = (f32[256]{0:T(256)S(1)}, f32[256]{0:T(256)}, u32[]{:S(2)}) copy-start(f32[256]{0:T(256)} %get-tuple-element.8) | copy-start | bytes 3076
  1059.4 0.9 copy-start.9
  1077.0 2.2 copy-start.7
  1077.0 4.8 copy-start.8
  1078.9 14.0 %copy-start.4 = (f32[20,8,32,256]{3,2,1,0:T(8,128)}, f32[20,8,32,256]{3,2,1,0:T(8,128)S(1)}, u32[]{:S(2)}) copy-start(f32[20,8,32,256]{3,2,1,0:T(8,128)S(1)} %copy.146) | copy-start | bytes 15728644
  1104.4 3.3 copy-start.2
  1117.5 16.6 %slice-start = ((s8[5242880]{0:T(1024)(128)(4,1)}), s8[1048576]{0:T(1024)(128)(4,1)S(1)}, s32[]{:S(2)}) async-start(s8[5242880]{0:T(1024)(128)(4,1)} %bitcast.351), calls=%async_computation.2 | async-start | bytes 2097152
  1125.4 8.8 slice-start.1
  1125.4 11.2 copy-start.6
  1158.5 3.3 copy-start.1
  1171.6 7.9 copy-start.10
  1171.6 16.6 %slice-start.2 = ((s8[5242880]{0:T(1024)(128)(4,1)}), s8[1048576]{0:T(1024)(128)(4,1)S(1)}, s32[]{:S(2)}) async-start(s8[5242880]{0:T(1024)(128)(4,1)} %bitcast.354), calls=%async_computation.4 | async-start | bytes 2097152
  1179.5 8.7 slice-start.3
  1179.5 11.0 copy-start.5
